TPU v7x, 32 devices: a whole 2x2x4 slice. The times are simulated.
32 devices in a mesh: groups: 2 (over y), seq: 4 (over z), chan: 2 (over x), rep: 2 (over core).
Axes of the slice: x: 2, y: 2, z: 4, core: 2. Of those that a mesh axis runs over, the one named last changes fastest.
Arguments:
- projected: bfloat16 [4096, 3, 8192], P(('groups', 'seq'), None, ('chan', 'rep')), parts along dimension 0, may hold values from -6 to 6
- short_weight: float32 [3, 3, 8192], P(None, None, ('chan', 'rep')), may hold values from -3.5 to 3.5
- skip_gain: float32 [8192], P(('chan', 'rep')), may hold values from -4 to 4
- pole_rate: float32 [16, 512], P(None, ('chan', 'rep')), may hold values from 2.4414062e-06 to 0.03
- residue: float32 [16, 512], P(None, ('chan', 'rep')), may hold values from -0.088388346 to 0.088388346
- out_weight: bfloat16 [2, 2, 2048, 4096], P(None, 'rep', 'seq', 'chan'), may hold values from -0.0625 to 0.0625
Outputs:
- mixed: bfloat16 [4096, 4096], P(('groups', 'seq'), ('chan', 'rep')), parts along dimension 0
There are 2 independent parts, one for each index of `groups`. A program takes and returns all parts, laid end to end along the dimension named above; an argument that names none is the same for every part. Nothing has to cross between parts.
All inputs are finite; a program needn't handle non-finite values.
Results may differ from a plain program's by a relative error of at most 0.005.
Values may be sent and summed in bfloat16 or wider, within the bound.
A program may use at most 128 MiB of HBM per device.

v0:
```python
import jax
import jax.numpy as jnp
from jax import lax
from jax.sharding import PartitionSpec as P

GROUP = 16
BLOCK = 128


def shifted(value, axis, steps):
    count = lax.axis_size(axis)
    initial, last = (max(0, -steps), min(count, count - steps))
    return lax.ppermute(value, axis, [(source, source + steps) for source in range(initial, last)])


def filter_tables(decay_rate, residue, block_len):
    offsets = jnp.arange(block_len, dtype=jnp.int32)
    lag_diff = offsets[:, None] - offsets[None, :]
    lag_float = jnp.maximum(lag_diff, 0).astype(decay_rate.dtype)
    kernel = jnp.zeros((decay_rate.shape[1], block_len, block_len), decay_rate.dtype)
    for order_idx in range(decay_rate.shape[0]):
        kernel = kernel + residue[order_idx][:, None, None] * jnp.exp(
            -decay_rate[order_idx][:, None, None] * lag_float[None]
        )
    kernel = jnp.where(lag_diff[None] >= 0, kernel, jnp.zeros_like(kernel))
    rate_t = decay_rate.T
    ahead = (offsets + 1).astype(decay_rate.dtype)
    readout = residue.T[:, None, :] * jnp.exp(-rate_t[:, None, :] * ahead[None, :, None])
    behind = (block_len - 1 - offsets).astype(decay_rate.dtype)
    intake = jnp.exp(-rate_t[:, :, None] * behind[None, None, :])
    return (kernel, readout, intake)


def block_conv(product, decay_rate, residue):
    groups = decay_rate.shape[1]
    group_size = product.shape[1] // groups
    kernel, readout, intake = filter_tables(decay_rate, residue, BLOCK)
    step_decay = jnp.exp(-decay_rate * BLOCK)[:, :, None]
    num_blocks = product.shape[0] // BLOCK
    blocks_in = product.reshape(num_blocks, BLOCK, groups, group_size)
    highest = lax.Precision.HIGHEST

    def block_step(carry_state, block_in):
        inside = jnp.einsum("gij,jgc->igc", kernel, block_in, precision=highest)
        across = jnp.einsum("gin,ngc->igc", readout, carry_state, precision=highest)
        updated = step_decay * carry_state + jnp.einsum(
            "gnj,jgc->ngc", intake, block_in, precision=highest
        )
        return (updated, inside + across)

    start_state = jnp.zeros((decay_rate.shape[0], groups, group_size), jnp.float32)
    final_state, outputs = lax.scan(block_step, start_state, blocks_in)
    return outputs.reshape(product.shape)


def per_device(projected, short_weight, skip_gain, pole_rate, residue, out_weight):
    tok_rows = projected.shape[0]
    chan_width = projected.shape[2]
    groups = pole_rate.shape[1]
    modes = pole_rate.shape[0]
    highest = lax.Precision.HIGHEST
    last_rows = projected[tok_rows - 2 :]
    earlier_rows = shifted(last_rows, "seq", 1)
    features = projected.astype(jnp.float32)
    extended = jnp.concatenate([earlier_rows.astype(jnp.float32), features], axis=0)
    filtered = (
        short_weight[:, 0][None] * features
        + short_weight[:, 1][None] * extended[1 : tok_rows + 1]
        + short_weight[:, 2][None] * extended[:tok_rows]
    )
    query_part = filtered[:, 0]
    product = filtered[:, 1] * filtered[:, 2]
    grouped = product.reshape(tok_rows, groups, GROUP)
    rate_t = pole_rate.T
    positions = jnp.arange(tok_rows, dtype=jnp.int32)
    end_weights = jnp.exp(
        -rate_t[:, :, None] * (tok_rows - 1 - positions).astype(jnp.float32)[None, None, :]
    )
    local_end = jnp.einsum("gnt,tgc->ngc", end_weights, grouped, precision=highest).reshape(
        modes, chan_width
    )
    channel_rate = jnp.repeat(pole_rate, GROUP, axis=1)
    my_index = lax.axis_index("seq")
    shard_piece = lax.all_gather(local_end[None], "seq", axis=0, tiled=True)
    shard_ids = jnp.arange(shard_piece.shape[0], dtype=jnp.int32)
    distance = my_index - 1 - shard_ids
    spans = (tok_rows * jnp.maximum(distance, 0)).astype(jnp.float32)
    factors = jnp.exp(-channel_rate[None] * spans[:, None, None])
    factors = jnp.where((distance >= 0)[:, None, None], factors, jnp.zeros_like(factors))
    prior = jnp.sum(factors * shard_piece, axis=0)
    local_conv = block_conv(product, pole_rate, residue)
    rise = residue.T[:, None, :] * jnp.exp(
        -rate_t[:, None, :] * (positions + 1).astype(jnp.float32)[None, :, None]
    )
    across = jnp.einsum(
        "gtn,ngc->tgc", rise, prior.reshape(modes, groups, GROUP), precision=highest
    ).reshape(tok_rows, chan_width)
    conv = local_conv + across
    gated_out = (query_part * (conv + skip_gain[None] * product)).astype(jnp.bfloat16)
    gathered = lax.all_gather(
        gated_out.reshape(tok_rows, 1, chan_width), "chan", axis=1, tiled=True
    )
    out_cols = out_weight.shape[3]
    partial_value = jnp.dot(
        gathered.reshape(tok_rows, -1),
        lax.all_gather(out_weight, "seq", axis=2, tiled=True).reshape(-1, out_cols),
        preferred_element_type=jnp.float32,
    )
    return lax.psum_scatter(partial_value, "rep", scatter_dimension=1, tiled=True).astype(
        jnp.bfloat16
    )


def solution(mesh):
    return jax.shard_map(
        per_device,
        mesh=mesh,
        in_specs=(
            P(("groups", "seq"), None, ("chan", "rep")),
            P(None, None, ("chan", "rep")),
            P(("chan", "rep")),
            P(None, ("chan", "rep")),
            P(None, ("chan", "rep")),
            P(None, "rep", "seq", "chan"),
        ),
        out_specs=P(("groups", "seq"), ("chan", "rep")),
        check_vma=False,
    )
```

profile of v0, /device:TPU:25, one launch (start us, length us, event | category | flops | bytes accessed | tf_op | source)
XLA Modules:
  0.0 770.3 jit_solution(116258044077898195)
XLA Ops:
  15.5 8.7 %copy.59 = bf16[512,3,2048]{0,2,1:T(8,128)(2,1)} copy(bf16[512,3,2048]{2,0,1:T(8,128)(2,1)} %param.8) | data formatting | bytes 12582912 | tf_op args[0]
  24.3 9.1 %convert_element_type.85 = f32[512,3,2048]{0,2,1:T(8,128)} convert(bf16[512,3,2048]{0,2,1:T(8,128)(2,1)} %copy.59) | non-fusion elementwise | flops 3145728 | bytes 18874368 | tf_op jit(solution)/shard_map/convert_element_type | solution.py:64
  37.3 18.0 %fusion.125 = f32[512,3,2048]{0,2,1:T(8,128)S(1)} fusion(f32[2,3,2048]{0,2,1:T(8,128)} %copy.60, f32[512,3,2048]{0,2,1:T(8,128)} %convert_element_type.85, f32[3,2048]{1,0:T(4,128)S(1)} %get-tuple-element.794, f32[3,2048]{1,0:T(4,128)S(1)} %get-tuple-element.795, f32[3,2048]{1,0:T(4,128)S(1)} %bitcast.135), kind=kLoop, calls=%fused_computation.127 | loop fusion | flops 22020096 | bytes 25288704 | tf_op jit(solution)/shard_map/add | solution.py:67
  55.3 4.5 copy-done
  62.7 5.3 mul.542
  68.0 278.8 %while.15 = (s32[]{:T(128)}, f32[16,128,16]{0,2,1:T(8,128)S(1)}, f32[4,128,128,16]{1,0,3,2:T(4,128)}, f32[16,128,1]{0,1,2:T(8,128)S(1)}, f32[4,128,128,16]{1,0,3...) while((s32[]{:T(128)}, f32[16,128,16]{0,2,1:T(8,128)S(1)}, ...), condition=%wide.region_1.2_spmd.clone.clone.clone, body=%wide.region_0.1_spmd.clone.clone.clone.sunk | while | flops 605159424 | bytes 9962904 | solution.py:52
  71.3 35.3 %fusion.167 = f32[128,16,128]{2,1,0:T(8,128)} fusion(f32[128,128,16]{0,2,1:T(8,128)S(1)} %bitcast.127, f32[128]{0:T(128)S(1)} %get-tuple-element.1185, f32[128]{0:T(128)S(1)} %get-tuple-element.1186, f32[128]{0:T(128)S(1)} %get-tuple-element.1182, f32[128]{0:T(128)S(1)} %get-tuple-element.1183, f32[128]{0:T(128)S(1)} %get-tuple-element.1180, ...), kind=kOutput, calls=%fused_computation.3.clone.1 | convolution fusion | flops 503316480 | bytes 2195456 | tf_op jit(solution)/shard_map/while/body/eval_jaxpr/gij,jgc->igc/dot_general | solution.py:44
  111.2 26.5 %dynamic_update_slice.8 = f32[4,128,128,16]{1,0,3,2:T(4,128)} dynamic-update-slice(f32[4,128,128,16]{1,0,3,2:T(4,128)} %get-tuple-element.1104, f32[1,128,128,16]{1,0,3,2:T(1,128)S(1)} %bitcast.126, s32[]{:T(128)S(6)} %copy.88, s32[]{:T(128)} %constant.16.clone.1..sunk, s32[]{:T(128)} %constant.16.clone.1..sunk, s32[]{:T(128)} %constant.16.clone.1..sunk) | dynamic-update-slice | bytes 2097156 | tf_op jit(solution)/shard_map/while/body/jit(dynamic_update_index_in_dim)/dynamic_update_slice | solution.py:52
  141.0 35.3 %fusion.167 = f32[128,16,128]{2,1,0:T(8,128)} fusion(f32[128,128,16]{0,2,1:T(8,128)S(1)} %bitcast.127, f32[128]{0:T(128)S(1)} %get-tuple-element.1185, f32[128]{0:T(128)S(1)} %get-tuple-element.1186, f32[128]{0:T(128)S(1)} %get-tuple-element.1182, f32[128]{0:T(128)S(1)} %get-tuple-element.1183, f32[128]{0:T(128)S(1)} %get-tuple-element.1180, ...), kind=kOutput, calls=%fused_computation.3.clone.1 | convolution fusion | flops 503316480 | bytes 2195456 | tf_op jit(solution)/shard_map/while/body/eval_jaxpr/gij,jgc->igc/dot_general | solution.py:44
  180.9 26.5 %dynamic_update_slice.8 = f32[4,128,128,16]{1,0,3,2:T(4,128)} dynamic-update-slice(f32[4,128,128,16]{1,0,3,2:T(4,128)} %get-tuple-element.1104, f32[1,128,128,16]{1,0,3,2:T(1,128)S(1)} %bitcast.126, s32[]{:T(128)S(6)} %copy.88, s32[]{:T(128)} %constant.16.clone.1..sunk, s32[]{:T(128)} %constant.16.clone.1..sunk, s32[]{:T(128)} %constant.16.clone.1..sunk) | dynamic-update-slice | bytes 2097156 | tf_op jit(solution)/shard_map/while/body/jit(dynamic_update_index_in_dim)/dynamic_update_slice | solution.py:52
  210.7 35.3 %fusion.167 = f32[128,16,128]{2,1,0:T(8,128)} fusion(f32[128,128,16]{0,2,1:T(8,128)S(1)} %bitcast.127, f32[128]{0:T(128)S(1)} %get-tuple-element.1185, f32[128]{0:T(128)S(1)} %get-tuple-element.1186, f32[128]{0:T(128)S(1)} %get-tuple-element.1182, f32[128]{0:T(128)S(1)} %get-tuple-element.1183, f32[128]{0:T(128)S(1)} %get-tuple-element.1180, ...), kind=kOutput, calls=%fused_computation.3.clone.1 | convolution fusion | flops 503316480 | bytes 2195456 | tf_op jit(solution)/shard_map/while/body/eval_jaxpr/gij,jgc->igc/dot_general | solution.py:44
  250.6 26.5 %dynamic_update_slice.8 = f32[4,128,128,16]{1,0,3,2:T(4,128)} dynamic-update-slice(f32[4,128,128,16]{1,0,3,2:T(4,128)} %get-tuple-element.1104, f32[1,128,128,16]{1,0,3,2:T(1,128)S(1)} %bitcast.126, s32[]{:T(128)S(6)} %copy.88, s32[]{:T(128)} %constant.16.clone.1..sunk, s32[]{:T(128)} %constant.16.clone.1..sunk, s32[]{:T(128)} %constant.16.clone.1..sunk) | dynamic-update-slice | bytes 2097156 | tf_op jit(solution)/shard_map/while/body/jit(dynamic_update_index_in_dim)/dynamic_update_slice | solution.py:52
  280.4 35.3 %fusion.167 = f32[128,16,128]{2,1,0:T(8,128)} fusion(f32[128,128,16]{0,2,1:T(8,128)S(1)} %bitcast.127, f32[128]{0:T(128)S(1)} %get-tuple-element.1185, f32[128]{0:T(128)S(1)} %get-tuple-element.1186, f32[128]{0:T(128)S(1)} %get-tuple-element.1182, f32[128]{0:T(128)S(1)} %get-tuple-element.1183, f32[128]{0:T(128)S(1)} %get-tuple-element.1180, ...), kind=kOutput, calls=%fused_computation.3.clone.1 | convolution fusion | flops 503316480 | bytes 2195456 | tf_op jit(solution)/shard_map/while/body/eval_jaxpr/gij,jgc->igc/dot_general | solution.py:44
  320.3 26.5 %dynamic_update_slice.8 = f32[4,128,128,16]{1,0,3,2:T(4,128)} dynamic-update-slice(f32[4,128,128,16]{1,0,3,2:T(4,128)} %get-tuple-element.1104, f32[1,128,128,16]{1,0,3,2:T(1,128)S(1)} %bitcast.126, s32[]{:T(128)S(6)} %copy.88, s32[]{:T(128)} %constant.16.clone.1..sunk, s32[]{:T(128)} %constant.16.clone.1..sunk, s32[]{:T(128)} %constant.16.clone.1..sunk) | dynamic-update-slice | bytes 2097156 | tf_op jit(solution)/shard_map/while/body/jit(dynamic_update_index_in_dim)/dynamic_update_slice | solution.py:52
  346.8 5.5 reshape.262
  352.3 6.8 fusion.133
  359.4 13.2 %all_gather.9 = f32[4,16,2048]{2,1,0:T(8,128)S(1)} all-gather(f32[1,16,2048]{2,1,0:T(8,128)S(1)} %copy.67), channel_id=1, replica_groups=mesh['groups'=2,'seq'=4,'chan'=2,'rep'=2] {'seq'}, dimensions={0}, use_global_device_ids=true | all-gather | bytes 655360 | tf_op jit(solution)/shard_map/all_gather | solution.py:84
  373.1 4.5 fusion.129
  377.6 6.4 fusion.127
  387.4 59.2 %all-gather.3.cloned.1.call-done = bf16[512,2,2048]{2,0,1:T(8,128)(2,1)} async-done(((bf16[512,1,2048]{2,0,1:T(8,128)(2,1)}), bf16[512,2,2048]{2,0,1:T(8,128)(2,1)}) %all-gather.3.cloned.1.call-update) | async-done | bytes 4194320 | tf_op jit(solution)/shard_map/all_gather | solution.py:100
  446.6 6.3 copy.71
  452.9 279.3 %all-gather.5.cloned.1.call-done = bf16[2,1,2048,2048]{3,2,1,0:T(8,128)(2,1)} async-done(((bf16[2,1,512,2048]{3,2,1,0:T(8,128)(2,1)}), bf16[2,1,2048,2048]{3,2,1,0:T(8,128)(2,1)}) %all-gather.5.cloned.1.call-update) | async-done | bytes 16777232 | tf_op jit(solution)/shard_map/all_gather | solution.py:106
  732.2 14.9 %fusion.145 = f32[512,2048]{1,0:T(8,128)} fusion(bf16[512,4096]{0,1:T(8,128)(2,1)} %bitcast.132, bf16[4096,2048]{1,0:T(8,128)(2,1)} %bitcast.136), kind=kOutput, calls=%fused_computation.197 | convolution fusion | flops 8589934592 | bytes 25165824 | tf_op jit(solution)/shard_map/dot_general | solution.py:104
  747.1 14.0 %reduce-scatter.2.cloned.1.call-done = f32[512,1024]{1,0:T(8,128)} async-done(((f32[512,2048]{1,0:T(8,128)}), f32[512,1024]{1,0:T(8,128)}) %reduce-scatter.2.cloned.1.call-update) | async-done | bytes 2097168 | tf_op jit(solution)/shard_map/reduce_scatter | solution.py:109
  (63 shorter events, 54.2 us)
Async XLA Ops:
  6.5 17.7 %copy-start.2 = (f32[16,128]{1,0:T(8,128)S(1)}, f32[16,128]{1,0:T(8,128)}, u32[]{:S(2)}) copy-start(f32[16,128]{1,0:T(8,128)} %param.12) | copy-start | bytes 24580
  6.5 440.1 %all-gather.3.cloned.1.call-start = ((), (), s32[]{:S(2)}) async-start(), calls=%async_computation.1 | async-start | bytes 6291456 | tf_op jit(solution)/shard_map/all_gather | solution.py:100
  7.5 27.8 %collective-permute-start = (bf16[2,3,2048]{2,0,1:T(2,128)(2,1)S(1)}, bf16[2,3,2048]{2,0,1:T(2,128)(2,1)S(1)}, u32[]{:S(2)}, u32[]{:S(2)}) collective-permute-start(bf16[2,3,2048]{2,0,1:T(2,128)(2,1)S(1)} %slice.125), channel_id=1, source_target_pairs={{0,4},{4,8},{8,12},{1,5},{5,9},{9,13},{2,6},{6,10},{10,14},{3,7},{... | collective-permute-start | bytes 73736 | tf_op jit(solution)/shard_map/ppermute | solution.py:13
  55.3 4.5 copy-start
  346.8 5.6 copy-start.4
  346.8 25.8 %copy-start.1 = (f32[16,2048]{1,0:T(8,128)S(1)}, f32[16,2048]{1,0:T(8,128)}, u32[]{:S(2)}) copy-start(f32[16,2048]{1,0:T(8,128)} %neg.232) | copy-start | bytes 393220
  346.8 25.8 %copy-start.6 = (f32[4]{0:T(128)S(1)}, f32[4]{0:T(128)}, u32[]{:S(2)}) copy-start(f32[4]{0:T(128)} %multiply_convert_fusion) | copy-start | bytes 52
  346.8 25.8 %copy-start.7 = (pred[4]{0:T(512)(128)(4,1)S(1)}, pred[4]{0:T(512)(128)(4,1)}, u32[]{:S(2)}) copy-start(pred[4]{0:T(512)(128)(4,1)} %fusion.142) | copy-start | bytes 16
  346.8 26.3 %copy-start.3 = (f32[512]{0:T(512)S(1)}, f32[512]{0:T(512)}, u32[]{:S(2)}) copy-start(f32[512]{0:T(512)} %add_convert_fusion) | copy-start | bytes 6148
  352.3 25.3 %copy-start.5 = (f32[2048]{0:T(1024)S(1)}, f32[2048]{0:T(1024)}, u32[]{:S(2)}) copy-start(f32[2048]{0:T(1024)} %param.10) | copy-start | bytes 24580
  386.6 345.6 %all-gather.5.cloned.1.call-start = ((), (), s32[]{:S(2)}) async-start(), calls=%async_computation.2 | async-start | bytes 20971520 | tf_op jit(solution)/shard_map/all_gather | solution.py:106
  387.3 373.7 %reduce-scatter.2.cloned.1.call-start = ((), (), s32[]{:S(2)}) async-start(), calls=%async_computation.3 | async-start | bytes 6291456 | tf_op jit(solution)/shard_map/reduce_scatter | solution.py:109
Sparse Core Ops, SparseCore 0:
  386.7 59.8 all-gather.2
  448.2 283.9 all-gather.4
  747.2 13.7 reduce-scatter.1
where the time goes:
time: 775 us; the launch traced here: 770 us
  waiting for transfers between devices  353 us (46%)
  matrix products  186 us (24%)
  local copies, waits for them, and re-layouts  160 us (21%)
  other arithmetic  43.3 us (6%)
  between operations  13.3 us (2%)
  blocking collectives  13.2 us (2%)
    all_gather x1, waiting for transfers between devices, per_device(): lax.all_gather(out_weight, 'seq', axis=2, tiled=True).reshape(-1, out_cols)  279 us
    dot_general x4, matrix products, block_step(): inside = jnp.einsum('gij,jgc->igc', kernel, block_in, precision=highest)  141 us
    dynamic_update_slice x4, local copies, waits for them, and re-layouts, block_conv(): final_state, outputs = lax.scan(block_step, start_state, blocks_in)  106 us
    all_gather x1, waiting for transfers between devices, per_device(): lax.all_gather(gated_out.reshape(tok_rows, 1, chan_width), 'chan', axis=1...  59.2 us
    add x1, other arithmetic, per_device(): short_weight[:, 0][None] * features  18 us
  transfers between devices with their start and end apart: 4, of which 3 were waited for; matrix products, arithmetic and copies ran while one was open for 4% of the time, Pallas kernels for 0%

commit v1 on v0

v1 whole, which is shorter than its diff:
```python
import functools

import jax
import jax.numpy as jnp
from jax import lax
from jax.experimental import pallas as pl
from jax.experimental.pallas import tpu as pltpu
from jax.sharding import PartitionSpec as P

GROUP = 16
LANES = 128
BLOCK = 128
PER_TILE = LANES // GROUP


def masked_rows(rows):
    lane_group = lax.broadcasted_iota(jnp.int32, rows.shape, 1) // GROUP
    zero = jnp.zeros_like(rows)
    return jnp.concatenate(
        [jnp.where(lane_group == g, rows, zero) for g in range(PER_TILE)], axis=0
    )


def readout_table(rate_row, res_row):
    ahead = (lax.broadcasted_iota(jnp.int32, (BLOCK, rate_row.shape[1]), 0) + 1).astype(jnp.float32)
    return res_row * jnp.exp(-rate_row * ahead)


def conv_body(x_ref, halo_ref, sw_ref, skip_ref, rate_rep_ref, res_rep_ref, rate_row_ref,
              res_row_ref, rate_ch_ref, q_ref, base_ref, end_ref, ext, lhs):
    tok = x_ref.shape[1]
    blocks = tok // BLOCK
    modes = rate_ch_ref.shape[0]

    def short(s):
        x = x_ref[s].astype(jnp.float32)
        ext[8:, :] = x
        ext[6:8, :] = halo_ref[s].astype(jnp.float32)
        return (
            sw_ref[s, 0:1, :] * x
            + sw_ref[s, 1:2, :] * ext[7 : tok + 7, :]
            + sw_ref[s, 2:3, :] * ext[6 : tok + 6, :]
        )

    q_ref[...] = short(0)
    product = short(1)
    product = product * short(2)

    lane = lax.broadcasted_iota(jnp.int32, rate_rep_ref.shape, 1) % BLOCK
    rate_rep = rate_rep_ref[...]
    back = ((BLOCK - lane) % BLOCK).astype(jnp.float32)
    row = jnp.sum(res_rep_ref[...] * jnp.exp(-rate_rep * back), axis=0, keepdims=True)
    lower = lax.broadcasted_iota(jnp.int32, (BLOCK, BLOCK), 1) <= lax.broadcasted_iota(
        jnp.int32, (BLOCK, BLOCK), 0
    )
    for g in range(PER_TILE):
        cols = slice(g * BLOCK, (g + 1) * BLOCK)
        wide = jnp.broadcast_to(row[:, cols], (BLOCK, BLOCK))
        table = pltpu.roll(wide, 0, 1, stride=1, stride_axis=0)
        lhs[:BLOCK, cols] = jnp.where(lower, table, 0.0).astype(jnp.bfloat16)
    lhs[BLOCK:, :] = jnp.exp(-rate_rep * (BLOCK - 1 - lane).astype(jnp.float32)).astype(jnp.bfloat16)

    decay = jnp.exp(-rate_ch_ref[...] * BLOCK)
    readout = readout_table(rate_row_ref[...], res_row_ref[...]).astype(jnp.bfloat16)
    state = jnp.zeros((modes, LANES), jnp.float32)
    for b in range(blocks):
        rows = slice(b * BLOCK, (b + 1) * BLOCK)
        p_b = product[rows]
        out = jnp.dot(lhs[...], masked_rows(p_b.astype(jnp.bfloat16)), preferred_element_type=jnp.float32)
        value = out[:BLOCK] + skip_ref[...] * p_b
        if b > 0:
            value = value + jnp.dot(
                readout, masked_rows(state.astype(jnp.bfloat16)), preferred_element_type=jnp.float32
            )
        base_ref[rows, :] = value
        state = decay * state + out[BLOCK:]
    end_ref[...] = state


def gate_body(q_ref, base_ref, prior_ref, rate_row_ref, res_row_ref, rate_ch_ref, out_ref):
    readout = readout_table(rate_row_ref[...], res_row_ref[...]).astype(jnp.bfloat16)
    decay = jnp.exp(-rate_ch_ref[...] * BLOCK)
    state = prior_ref[...]
    for b in range(q_ref.shape[0] // BLOCK):
        rows = slice(b * BLOCK, (b + 1) * BLOCK)
        across = jnp.dot(
            readout, masked_rows(state.astype(jnp.bfloat16)), preferred_element_type=jnp.float32
        )
        out_ref[rows, :] = (q_ref[rows, :] * (base_ref[rows, :] + across)).astype(jnp.bfloat16)
        state = decay * state


def project_body(a_ref, w_ref, out_ref):
    @pl.when((pl.program_id(1) == 0) & (pl.program_id(2) == 0))
    def _():
        out_ref[...] = jnp.zeros_like(out_ref)

    w = w_ref[...].reshape(-1, w_ref.shape[-1])
    out_ref[...] += jnp.dot(a_ref[0], w, preferred_element_type=jnp.float32)


def per_device(projected, short_weight, skip_gain, pole_rate, residue, out_weight):
    tok = projected.shape[0]
    chans = projected.shape[2]
    modes, groups = pole_rate.shape
    tiles = chans // LANES
    count = lax.axis_size("seq")
    slabs = lax.axis_size("groups")
    n_chan = out_weight.shape[0]
    local_rows = out_weight.shape[2]
    out_cols = out_weight.shape[3]
    half = out_cols // slabs
    wide = PER_TILE * BLOCK

    mine = lax.dynamic_slice_in_dim(
        out_weight[:, 0], lax.axis_index("groups") * half, half, axis=2
    )
    weight = lax.all_gather(mine, ("groups", "seq"), axis=0)
    weight = weight.reshape(slabs, count, n_chan, local_rows, half)

    x = projected.transpose(1, 0, 2)
    halo = lax.ppermute(x[:, tok - 2 :], "seq", [(i, i + 1) for i in range(count - 1)])
    rate_rep = jnp.repeat(pole_rate, BLOCK, axis=1)
    res_rep = jnp.repeat(residue, BLOCK, axis=1)
    rate_row = pole_rate.T.reshape(1, -1)
    res_row = residue.T.reshape(1, -1)
    rate_ch = jnp.repeat(pole_rate, GROUP, axis=1)

    def spec(*lead, width=LANES):
        return pl.BlockSpec((*lead, width), lambda t: (0,) * len(lead) + (t,))

    q, base, end = pl.pallas_call(
        conv_body,
        grid=(tiles,),
        in_specs=[
            spec(3, tok), spec(3, 2), spec(3, 3), spec(1), spec(modes, width=wide),
            spec(modes, width=wide), spec(1), spec(1), spec(modes),
        ],
        out_specs=[spec(tok), spec(tok), spec(modes)],
        out_shape=[
            jax.ShapeDtypeStruct((tok, chans), jnp.float32),
            jax.ShapeDtypeStruct((tok, chans), jnp.float32),
            jax.ShapeDtypeStruct((modes, chans), jnp.float32),
        ],
        scratch_shapes=[
            pltpu.VMEM((tok + 8, LANES), jnp.float32),
            pltpu.VMEM((BLOCK + modes, wide), jnp.bfloat16),
        ],
        cost_estimate=pl.CostEstimate(
            flops=2 * tok * chans * 1152, bytes_accessed=14 * tok * chans, transcendentals=0
        ),
        name="conv_local",
    )(x, halo, short_weight, skip_gain[None], rate_rep, res_rep, rate_row, res_row, rate_ch)

    ends = lax.all_gather(end, "seq", axis=0)
    distance = lax.axis_index("seq") - 1 - jnp.arange(count, dtype=jnp.int32)
    spans = (tok * jnp.maximum(distance, 0)).astype(jnp.float32)
    factors = jnp.exp(-rate_ch[None] * spans[:, None, None])
    prior = jnp.sum(jnp.where((distance >= 0)[:, None, None], factors * ends, 0.0), axis=0)

    gated = pl.pallas_call(
        gate_body,
        grid=(tiles,),
        in_specs=[spec(tok), spec(tok), spec(modes), spec(1), spec(1), spec(modes)],
        out_specs=spec(tok),
        out_shape=jax.ShapeDtypeStruct((tok, chans), jnp.bfloat16),
        cost_estimate=pl.CostEstimate(
            flops=2 * tok * chans * 128, bytes_accessed=10 * tok * chans, transcendentals=0
        ),
        name="gate",
    )(q, base, prior, rate_row, res_row, rate_ch)

    full = lax.all_gather(gated, "chan", axis=0)
    step = max(1, LANES // local_rows)
    depth = step * local_rows
    partial_sum = pl.pallas_call(
        project_body,
        grid=(slabs, n_chan, count // step),
        in_specs=[
            pl.BlockSpec((1, tok, depth), lambda g, c, s: (c, 0, s)),
            pl.BlockSpec((1, step, 1, local_rows, half), lambda g, c, s: (g, s, c, 0, 0)),
        ],
        out_specs=pl.BlockSpec((tok, half), lambda g, c, s: (0, g)),
        out_shape=jax.ShapeDtypeStruct((tok, out_cols), jnp.float32),
        cost_estimate=pl.CostEstimate(
            flops=2 * tok * n_chan * chans * out_cols,
            bytes_accessed=2 * n_chan * chans * out_cols + 4 * tok * out_cols,
            transcendentals=0,
        ),
        name="project",
    )(full, weight)
    return lax.psum_scatter(partial_sum, "rep", scatter_dimension=1, tiled=True).astype(
        jnp.bfloat16
    )


def solution(mesh):
    return jax.shard_map(
        per_device,
        mesh=mesh,
        in_specs=(
            P(("groups", "seq"), None, ("chan", "rep")),
            P(None, None, ("chan", "rep")),
            P(("chan", "rep")),
            P(None, ("chan", "rep")),
            P(None, ("chan", "rep")),
            P(None, "rep", "seq", "chan"),
        ),
        out_specs=P(("groups", "seq"), ("chan", "rep")),
        check_vma=False,
    )
```

time: 775 us -> 394 us (0.51)
  matrix products: 186 us -> 0 us
  local copies, waits for them, and re-layouts: 160 us -> 11.9 us
  waiting for transfers between devices: 353 us -> 298 us
  Pallas kernels: 0 us -> 50.4 us
  other arithmetic: 43.3 us -> 3.57 us
    dot_general x15 -> x0, matrix products: 186 us -> none  [the longest x4 141 us: block_step(): inside = jnp.einsum('gij,jgc->igc', kernel, block_in, precision=highest)]
    dynamic_update_slice x4 -> x0, local copies, waits for them, and re-layouts: 106 us -> none  [block_conv(): final_state, outputs = lax.scan(block_step, start_state, blocks_in)]
    all_gather x2, waiting for transfers between devices: 339 us -> 285 us  [the longest x1 228 us: per_device(): weight = lax.all_gather(mine, ('groups', 'seq'), axis=0)]
    pallas_call x0 -> x3, Pallas kernels: none -> 50.4 us  [the longest x1 20.6 us: per_device(): pl.pallas_call(project_body, grid=(slabs, n_chan, count // step), in_spec...]
    add x1 -> x0, other arithmetic: 18 us -> none  [per_device(): short_weight[:, 0][None] * features]
    convert_element_type x8 -> x2, other arithmetic: 19.9 us -> 2.73 us  [the longest x1 2.72 us: per_device(): lax.psum_scatter(partial_sum, 'rep', scatter_dimension=1, tiled=True)]
    unnamed x22 -> x8, local copies, waits for them, and re-layouts: 13.6 us -> 0.61 us
    dynamic_slice x4 -> x1, local copies, waits for them, and re-layouts: 13.3 us -> 3.11 us  [per_device(): lax.dynamic_slice_in_dim(out_weight[:, 0], lax.axis_index('groups') * hal...]
  transfers between devices with their start and end apart: 4 -> 4, of which waited for: 3 -> 3; matrix products, arithmetic and copies ran while one was open for 4% -> 3% of each run, Pallas kernels for 0% -> 0%
where the time goes in v1:
time: 394 us; the launch traced here: 392 us
  waiting for transfers between devices  298 us (76%)
  Pallas kernels  50.4 us (13%)
  blocking collectives  13.4 us (3%)
  between operations  13.2 us (3%)
  local copies, waits for them, and re-layouts  11.9 us (3%)
    all_gather x1, waiting for transfers between devices, per_device(): weight = lax.all_gather(mine, ('groups', 'seq'), axis=0)  228 us
    all_gather x1, waiting for transfers between devices, per_device(): full = lax.all_gather(gated, 'chan', axis=0)  56.8 us
    pallas_call x1, Pallas kernels, per_device(): pl.pallas_call(project_body, grid=(slabs, n_chan, count // step), in_spec...  20.6 us
    pallas_call x1, Pallas kernels, per_device(): pl.pallas_call(conv_body, grid=(tiles,), in_specs=[spec(3, tok), spec(3,...  17.9 us
    all_gather x1, blocking collectives, per_device(): ends = lax.all_gather(end, 'seq', axis=0)  13.4 us
    reduce_scatter x1, waiting for transfers between devices, per_device(): lax.psum_scatter(partial_sum, 'rep', scatter_dimension=1, tiled=True)  12.8 us
    pallas_call x1, Pallas kernels, per_device(): pl.pallas_call(gate_body, grid=(tiles,), in_specs=[spec(tok), spec(tok),...  11.9 us
  transfers between devices with their start and end apart: 4, of which 3 were waited for; matrix products, arithmetic and copies ran while one was open for 3% of the time, Pallas kernels for 0%

profile of v1, /device:TPU:25, one launch (start us, length us, event | category | flops | bytes accessed | tf_op | source)
XLA Modules:
  0.0 391.5 jit_solution(11257087990483536350)
XLA Ops:
  6.5 0.9 slice.4
  7.5 1.3 collective-permute-start
  8.8 1.0 broadcast_in_dim.27
  9.8 1.0 broadcast_in_dim.28
  10.9 2.6 copy_bitcast_fusion
  13.5 0.3 broadcast_in_dim.29
  13.8 0.6 reshape.41.rate_ch_ref
  14.5 0.1 copy.11
  14.6 0.7 reshape.39.rate_row_ref
  15.3 0.1 copy.12
  15.4 0.7 reshape.40.res_row_ref
  16.1 0.6 copy-done.3
  16.7 17.9 %conv_local.1 = (f32[512,2048]{1,0:T(8,128)}, f32[512,2048]{1,0:T(8,128)}, f32[16,2048]{1,0:T(8,128)}) custom-call(bf16[3,512,2048]{2,1,0:T(8,128)(2,1)} %bitcast.19, bf16[3,2,2048]{2,1,0:T(2,128)(2,1)} %copy-done.3, f32[3,3,2048]{2,1,0:T(4,128)} %sw_ref.1, f32[1,2048]{1,0:T(1,128)} %bitcast.22, f32[16,16384]{1,0:T(8,128)} %get-tuple-element.12.rate_rep_ref, ...), custom_call_target="tpu_custom_call" | custom-call | flops 2415919104 | bytes 14680064 | tf_op jit(solution)/shard_map/conv_local/pallas_call | solution.py:132
  34.6 13.4 %all-gather = f32[64,2048]{1,0:T(8,128)S(1)} all-gather(f32[16,2048]{1,0:T(8,128)} %get-tuple-element.10), channel_id=2, replica_groups=mesh['groups'=2,'seq'=4,'chan'=2,'rep'=2] {'seq'}, dimensions={0}, use_global_device_ids=true | all-gather | bytes 655360 | tf_op jit(solution)/shard_map/all_gather | solution.py:155
  48.0 0.8 select_reduce_fusion.prior_ref
  48.9 11.9 %gate.1 = bf16[512,2048]{1,0:T(8,128)(2,1)} custom-call(f32[512,2048]{1,0:T(8,128)} %get-tuple-element.8.q_ref, f32[512,2048]{1,0:T(8,128)} %get-tuple-element.9.base_ref, f32[16,2048]{1,0:T(8,128)} %select_reduce_fusion.prior_ref, f32[1,2048]{1,0:T(1,128)} %reshape.39.rate_row_ref, f32[1,2048]{1,0:T(1,128)} %reshape.40.res_row_ref, f32[16,2048]{1,0:T(8,128)} %copy-done), custom_call_target="tpu_custom_call" | custom-call | flops 268435456 | bytes 10485760 | tf_op jit(solution)/shard_map/gate/pallas_call | solution.py:161
  60.8 0.0 all-gather.8.cloned.1.call-start
  60.8 3.1 constant_dynamic-slice_fusion
  64.0 0.0 reduce-scatter.2.cloned.1.call-start
  64.0 56.8 %all-gather.6.cloned.1.call-done = bf16[1024,2048]{1,0:T(8,128)(2,1)} async-done(((bf16[512,2048]{1,0:T(8,128)(2,1)}), bf16[1024,2048]{1,0:T(8,128)(2,1)}) %all-gather.6.cloned.1.call-update) | async-done | bytes 4194320 | tf_op jit(solution)/shard_map/all_gather | solution.py:173
  120.8 228.0 %all-gather.8.cloned.1.call-done = bf16[16,1,512,1024]{3,2,1,0:T(8,128)(2,1)} async-done(((bf16[2,1,512,1024]{3,2,1,0:T(8,128)(2,1)}), bf16[16,1,512,1024]{3,2,1,0:T(8,128)(2,1)}) %all-gather.8.cloned.1.call-update) | async-done | bytes 16777232 | tf_op jit(solution)/shard_map/all_gather | solution.py:118
  348.8 20.6 %project.1 = f32[512,2048]{1,0:T(8,128)} custom-call(bf16[2,512,2048]{2,1,0:T(8,128)(2,1)} %bitcast.21, bf16[2,4,2,512,1024]{4,3,2,1,0:T(8,128)(2,1)} %bitcast.20), custom_call_target="tpu_custom_call" | custom-call | flops 8589934592 | bytes 20971520 | tf_op jit(solution)/shard_map/project/pallas_call | solution.py:176
  369.5 12.8 %reduce-scatter.2.cloned.1.call-done = f32[512,1024]{1,0:T(8,128)} async-done(((f32[512,2048]{1,0:T(8,128)}), f32[512,1024]{1,0:T(8,128)}) %reduce-scatter.2.cloned.1.call-update) | async-done | bytes 2097168 | tf_op jit(solution)/shard_map/reduce_scatter | solution.py:192
  382.3 2.7 convert_element_type.11
  (15 shorter events, 0.1 us)
Async XLA Ops:
  6.5 7.0 %copy-start.1 = (f32[16,128]{1,0:T(8,128)S(1)}, f32[16,128]{1,0:T(8,128)}, u32[]{:S(2)}) copy-start(f32[16,128]{1,0:T(8,128)} %param.9) | copy-start | bytes 24580
  6.5 114.3 %all-gather.6.cloned.1.call-start = ((), (), s32[]{:S(2)}) async-start(), calls=%async_computation.2 | async-start | bytes 6291456 | tf_op jit(solution)/shard_map/all_gather | solution.py:173
  7.5 8.6 %collective-permute-start = (bf16[3,2,2048]{2,1,0:T(2,128)(2,1)S(1)}, bf16[3,2,2048]{2,1,0:T(2,128)(2,1)S(1)}, u32[]{:S(2)}, u32[]{:S(2)}) collective-permute-start(bf16[3,2,2048]{2,1,0:T(2,128)(2,1)S(1)} %slice.4), channel_id=1, source_target_pairs={{0,4},{4,8},{8,12},{1,5},{5,9},{9,13},{2,6},{6,10},{10,14},{3,7},{... | collective-permute-start | bytes 73736 | tf_op jit(solution)/shard_map/ppermute | solution.py:122
  8.8 6.5 %copy-start.2 = (f32[16,128]{1,0:T(8,128)S(1)}, f32[16,128]{1,0:T(8,128)}, u32[]{:S(2)}) copy-start(f32[16,128]{1,0:T(8,128)} %param.10) | copy-start | bytes 24580
  14.5 1.6 copy-start
  16.1 0.6 copy-start.3
  60.8 288.1 %all-gather.8.cloned.1.call-start = ((), (), s32[]{:S(2)}) async-start(), calls=%async_computation.3 | async-start | bytes 18874368 | tf_op jit(solution)/shard_map/all_gather | solution.py:118
  64.0 318.3 %reduce-scatter.2.cloned.1.call-start = ((), (), s32[]{:S(2)}) async-start(), calls=%async_computation.1 | async-start | bytes 6291456 | tf_op jit(solution)/shard_map/reduce_scatter | solution.py:192
Sparse Core Ops, SparseCore 0:
  60.9 59.8 all-gather.5
  122.9 225.8 all-gather.7
  369.6 12.6 reduce-scatter.1

commit v2 on v0

v2 whole, which is shorter than its diff:
```python
import functools

import jax
import jax.numpy as jnp
from jax import lax
from jax.experimental import pallas as pl
from jax.experimental.pallas import tpu as pltpu
from jax.sharding import PartitionSpec as P

GROUP = 16
LANES = 128
BLOCK = 128
PER_TILE = LANES // GROUP
WIDE = PER_TILE * BLOCK
HALO = 16
MESH = pl.DeviceIdType.MESH
HIGHEST = lax.Precision.HIGHEST


def iota(shape, dim):
    return lax.broadcasted_iota(jnp.int32, shape, dim)


def masked_rows(rows):
    lane_group = iota(rows.shape, 1) // GROUP
    zero = jnp.zeros_like(rows)
    return jnp.concatenate(
        [jnp.where(lane_group == g, rows, zero) for g in range(PER_TILE)], axis=0
    )


def kernel(dims, x_hbm, sw_ref, skip_ref, rate_ref, res_ref, w_hbm, out_ref,
           xbuf, halo, ext, lhs, q_buf, base, ends, own_end, prior, rate_ch, readout, gated, wbuf,
           acc, peer, local_sem, halo_sem, end_send, end_recv, gate_send, gate_recv,
           zsend, zrecv, ysend, yrecv, rep_send, rep_recv):
    count, slabs, n_chan, n_rep, chunks, row_chunks = dims
    tok, chans = gated.shape[1], gated.shape[2]
    modes, groups = rate_ref.shape
    tiles = chans // LANES
    blocks = tok // BLOCK
    local_rows, out_cols = w_hbm.shape[2], w_hbm.shape[3]
    half = out_cols // slabs
    rows = local_rows // row_chunks
    out_half = out_cols // n_rep
    slab = lax.axis_index("groups")
    seq = lax.axis_index("seq")
    chan = lax.axis_index("chan")
    rep = lax.axis_index("rep")
    other_slab = 1 - slab
    other_rep = 1 - rep

    barrier = pltpu.get_barrier_semaphore()

    def greet(target):
        pl.semaphore_signal(barrier, inc=1, device_id=target, device_id_type=MESH)

    for d in range(1, count):
        greet({"seq": lax.rem(seq + d, count)})
    for d in range(1, n_chan):
        greet({"chan": lax.rem(chan + d, n_chan)})
    greet({"groups": other_slab})
    greet({"rep": other_rep})
    pl.semaphore_wait(barrier, count + n_chan)

    def piece(ref, c, r, h):
        cols = pl.ds(pl.multiple_of(h * half, LANES), half)
        if chunks == 1:
            return ref.at[:, :, cols]
        return ref.at[c, pl.ds(pl.multiple_of(r * rows, rows), rows), cols]

    def split(ch):
        return ch // row_chunks, ch % row_chunks

    def own_piece(ch):
        c, r = split(ch)
        return piece(w_hbm.at[:, 0], c, r, slab)

    def block_piece(b, ch, h):
        c, r = split(ch)
        return piece(wbuf.at[b], c, r, h)

    def target_of(direction):
        return seq + 1 if direction == 0 else seq - 1

    def can_send(direction):
        return seq < count - 1 if direction == 0 else seq > 0

    def origin(direction, k):
        return seq - 1 - k if direction == 0 else seq + 1 + k

    def has(direction, k):
        return seq - 1 - k >= 0 if direction == 0 else seq + 1 + k < count

    def z_copy(direction, k, ch, src, b):
        return pltpu.make_async_remote_copy(
            src_ref=src, dst_ref=block_piece(b, ch, slab),
            send_sem=zsend.at[direction, k, ch], recv_sem=zrecv.at[direction, k, ch],
            device_id={"seq": target_of(direction)}, device_id_type=MESH,
        )

    def y_copy(direction, k, ch, h):
        b = origin(direction, k)
        ref = block_piece(b, ch, h)
        return pltpu.make_async_remote_copy(
            src_ref=ref, dst_ref=ref,
            send_sem=ysend.at[direction, k, ch], recv_sem=yrecv.at[direction, k, ch],
            device_id={"groups": other_slab}, device_id_type=MESH,
        )

    def halo_copy():
        return pltpu.make_async_remote_copy(
            src_ref=x_hbm.at[:, pl.ds(tok - HALO, HALO), :], dst_ref=halo,
            send_sem=halo_sem.at[0], recv_sem=halo_sem.at[1],
            device_id={"seq": seq + 1}, device_id_type=MESH,
        )

    @pl.when(seq < count - 1)
    def _():
        halo_copy().start()

    for ch in range(chunks):
        for direction in (0, 1):
            @pl.when(can_send(direction))
            def _():
                z_copy(direction, 0, ch, own_piece(ch), seq).start()

    x_copy = pltpu.make_async_copy(x_hbm, xbuf, local_sem.at[0])
    x_copy.start()
    w_copy = pltpu.make_async_copy(w_hbm.at[:, 0], wbuf.at[seq], local_sem.at[1])
    w_copy.start()
    x_copy.wait()

    @pl.when(seq > 0)
    def _():
        halo_copy().wait_recv()

    @pl.when(seq == 0)
    def _():
        halo[...] = jnp.zeros_like(halo)

    def pump(k, ch):
        for direction in (0, 1):
            @pl.when(has(direction, k))
            def _():
                b = origin(direction, k)
                landed = block_piece(b, ch, slab)
                z_copy(direction, k, ch, landed, b).wait_recv()
                y_copy(direction, k, ch, slab).start()

                @pl.when(can_send(direction))
                def _():
                    z_copy(direction, k + 1, ch, landed, b).start()

    def conv_tile(t, carry):
        cols = pl.ds(pl.multiple_of(t * LANES, LANES), LANES)

        def short(s):
            x = xbuf[s, :, cols].astype(jnp.float32)
            ext[HALO:, :] = x
            ext[:HALO, :] = halo[s, :, cols].astype(jnp.float32)
            return (
                sw_ref[s, 0:1, cols] * x
                + sw_ref[s, 1:2, cols] * ext[HALO - 1 : tok + HALO - 1, :]
                + sw_ref[s, 2:3, cols] * ext[HALO - 2 : tok + HALO - 2, :]
            )

        q_buf[:, cols] = short(0)
        product = short(1)
        product = product * short(2)

        pick_wide = (
            iota((groups, WIDE), 0) == t * PER_TILE + iota((groups, WIDE), 1) // BLOCK
        ).astype(jnp.float32)
        pick = (
            iota((groups, LANES), 0) == t * PER_TILE + iota((groups, LANES), 1) // GROUP
        ).astype(jnp.float32)

        def spread(table, which):
            return jnp.dot(table, which, precision=HIGHEST, preferred_element_type=jnp.float32)

        rate, res = rate_ref[...], res_ref[...]
        rate_rep, res_rep = spread(rate, pick_wide), spread(res, pick_wide)
        rate_c, res_c = spread(rate, pick), spread(res, pick)
        diagonal = iota((modes, LANES), 0) == iota((modes, LANES), 1) % GROUP
        rate_row = jnp.sum(jnp.where(diagonal, rate_c, 0.0), axis=0, keepdims=True)
        res_row = jnp.sum(jnp.where(diagonal, res_c, 0.0), axis=0, keepdims=True)
        ahead = (iota((BLOCK, LANES), 0) + 1).astype(jnp.float32)
        read = (res_row * jnp.exp(-rate_row * ahead)).astype(jnp.bfloat16)

        lane = iota((modes, WIDE), 1) % BLOCK
        back = ((BLOCK - lane) % BLOCK).astype(jnp.float32)
        row = jnp.sum(res_rep * jnp.exp(-rate_rep * back), axis=0, keepdims=True)
        lower = iota((BLOCK, BLOCK), 1) <= iota((BLOCK, BLOCK), 0)
        for g in range(PER_TILE):
            part = slice(g * BLOCK, (g + 1) * BLOCK)
            wide = jnp.broadcast_to(row[:, part], (BLOCK, BLOCK))
            table = pltpu.roll(wide, 0, 1, stride=1, stride_axis=0)
            lhs[:BLOCK, part] = jnp.where(lower, table, 0.0).astype(jnp.bfloat16)
        lhs[BLOCK:, :] = jnp.exp(-rate_rep * (BLOCK - 1 - lane).astype(jnp.float32)).astype(
            jnp.bfloat16
        )

        decay = jnp.exp(-rate_c * BLOCK)
        state = jnp.zeros((modes, LANES), jnp.float32)
        for b in range(blocks):
            rows_b = slice(b * BLOCK, (b + 1) * BLOCK)
            p_b = product[rows_b]
            made = jnp.dot(
                lhs[...], masked_rows(p_b.astype(jnp.bfloat16)), preferred_element_type=jnp.float32
            )
            value = made[:BLOCK] + skip_ref[:, cols] * p_b
            if b > 0:
                value = value + jnp.dot(
                    read, masked_rows(state.astype(jnp.bfloat16)), preferred_element_type=jnp.float32
                )
            base[rows_b, cols] = value
            state = decay * state + made[BLOCK:]
        own_end[:, cols] = state
        rate_ch[:, cols] = rate_c
        readout[:, cols] = read
        return carry

    steps = [(k, ch) for k in range(count - 1) for ch in range(chunks)]
    early = 3 if len(steps) > 3 and chunks >= 3 else 1
    part = tiles // (early + 1)
    for e in range(early + 1):
        stop = tiles if e == early else (e + 1) * part
        lax.fori_loop(e * part, stop, conv_tile, 0)
        if e < early:
            pump(*steps[e])

    def end_copy(d):
        return pltpu.make_async_remote_copy(
            src_ref=own_end, dst_ref=ends.at[seq],
            send_sem=end_send.at[d], recv_sem=end_recv.at[seq],
            device_id={"seq": seq + d}, device_id_type=MESH,
        )

    def arrived_end(source):
        return pltpu.make_async_remote_copy(
            src_ref=own_end, dst_ref=ends.at[source],
            send_sem=end_send.at[0], recv_sem=end_recv.at[source],
            device_id={"seq": seq - 1}, device_id_type=MESH,
        )

    for d in range(1, count):
        @pl.when(seq + d < count)
        def _():
            end_copy(d).start()

    prior[...] = jnp.zeros_like(prior)
    for source in range(count - 1):
        @pl.when(source < seq)
        def _():
            arrived_end(source).wait_recv()
            prior[...] = prior[...] * jnp.exp(-rate_ch[...] * tok) + ends[source]

    def gate_tile(t, carry):
        cols = pl.ds(pl.multiple_of(t * LANES, LANES), LANES)
        read = readout[:, cols]
        decay = jnp.exp(-rate_ch[:, cols] * BLOCK)
        state = prior[:, cols]
        for b in range(blocks):
            rows_b = slice(b * BLOCK, (b + 1) * BLOCK)
            across = jnp.dot(
                read, masked_rows(state.astype(jnp.bfloat16)), preferred_element_type=jnp.float32
            )
            gated[chan, rows_b, cols] = (
                q_buf[rows_b, cols] * (base[rows_b, cols] + across)
            ).astype(jnp.bfloat16)
            state = decay * state
        return carry

    lax.fori_loop(0, tiles, gate_tile, 0)

    def gate_copy(d):
        return pltpu.make_async_remote_copy(
            src_ref=gated.at[chan], dst_ref=gated.at[chan],
            send_sem=gate_send.at[d], recv_sem=gate_recv.at[chan],
            device_id={"chan": lax.rem(chan + d, n_chan)}, device_id_type=MESH,
        )

    def arrived_gate(d):
        source = lax.rem(chan + d, n_chan)
        return pltpu.make_async_remote_copy(
            src_ref=gated.at[source], dst_ref=gated.at[source],
            send_sem=gate_send.at[0], recv_sem=gate_recv.at[source],
            device_id={"chan": source}, device_id_type=MESH,
        )

    for d in range(1, n_chan):
        gate_copy(d).start()

    middle = min(len(steps), early + 3)
    for e in range(early, middle):
        pump(*steps[e])
    acc[...] = jnp.zeros_like(acc)
    w_copy.wait()
    for d in range(1, n_chan):
        arrived_gate(d).wait_recv()

    streamed = chunks > 1
    col_tile = min(512, out_cols)

    def multiply(b, ch):
        c, r = split(ch)
        a = gated[c, :, pl.ds(pl.multiple_of(b * local_rows + r * rows, LANES), rows)]

        def column(n, carry):
            cols = pl.ds(pl.multiple_of(n * col_tile, col_tile), col_tile)
            w = wbuf[b, c, pl.ds(pl.multiple_of(r * rows, rows), rows), cols]
            acc[:, cols] += jnp.dot(a, w, preferred_element_type=jnp.float32)
            return carry

        lax.fori_loop(0, out_cols // col_tile, column, 0)

    def consume(k, ch):
        for direction in (0, 1):
            @pl.when(has(direction, k))
            def _():
                y_copy(direction, k, ch, other_slab).wait_recv()
                if streamed:
                    multiply(origin(direction, k), ch)

    if streamed:
        lax.fori_loop(0, chunks, lambda ch, carry: (multiply(seq, ch), carry)[1], 0)

    def both(j, carry):
        pump(j // chunks, j % chunks)
        old = j - 1
        consume(old // chunks, old % chunks)
        return carry

    def only(j, carry):
        consume(j // chunks, j % chunks)
        return carry

    total = len(steps)
    lax.fori_loop(0, middle - 1, only, 0)
    lax.fori_loop(middle, total, both, 0)
    lax.fori_loop(total - 1, total, only, 0)

    if not streamed:
        def whole_column(n, carry):
            cols = pl.ds(pl.multiple_of(n * half, half), half)
            for c in range(n_chan):
                w = wbuf[:, c, :, cols].reshape(count * local_rows, half)
                acc[:, cols] += jnp.dot(gated[c], w, preferred_element_type=jnp.float32)
            return carry

        lax.fori_loop(0, slabs, whole_column, 0)

    quarter = tok // 4

    def rep_copy(i, side):
        return pltpu.make_async_remote_copy(
            src_ref=acc.at[
                pl.ds(i * quarter, quarter), pl.ds(pl.multiple_of(side * out_half, LANES), out_half)
            ],
            dst_ref=peer.at[pl.ds(i * quarter, quarter), :],
            send_sem=rep_send.at[i], recv_sem=rep_recv.at[i],
            device_id={"rep": other_rep}, device_id_type=MESH,
        )

    for i in range(4):
        rep_copy(i, other_rep).start()
    mine = pl.ds(pl.multiple_of(rep * out_half, LANES), out_half)
    for i in range(4):
        rep_copy(i, other_rep).wait_recv()
        rows_i = pl.ds(i * quarter, quarter)
        out_ref[rows_i, :] = (acc[rows_i, mine] + peer[rows_i, :]).astype(jnp.bfloat16)

    for i in range(4):
        rep_copy(i, other_rep).wait_send()
    for d in range(1, n_chan):
        gate_copy(d).wait_send()
    for d in range(1, count):
        @pl.when(seq + d < count)
        def _():
            end_copy(d).wait_send()

    @pl.when(seq < count - 1)
    def _():
        halo_copy().wait_send()

    for ch in range(chunks):
        for direction in (0, 1):
            @pl.when(can_send(direction))
            def _():
                z_copy(direction, 0, ch, own_piece(ch), seq).wait_send()

    def drain(j, carry):
        k, ch = j // chunks, j % chunks
        for direction in (0, 1):
            @pl.when(has(direction, k))
            def _():
                y_copy(direction, k, ch, slab).wait_send()

                @pl.when(can_send(direction))
                def _():
                    b = origin(direction, k)
                    z_copy(direction, k + 1, ch, block_piece(b, ch, slab), b).wait_send()
        return carry

    lax.fori_loop(0, total, drain, 0)


def per_device(projected, short_weight, skip_gain, pole_rate, residue, out_weight):
    tok, _, chans = projected.shape
    modes, groups = pole_rate.shape
    n_chan, _, local_rows, out_cols = out_weight.shape
    count, slabs = lax.axis_size("seq"), lax.axis_size("groups")
    n_rep = lax.axis_size("rep")
    row_chunks = max(1, local_rows // 256)
    chunks = n_chan * row_chunks if local_rows % LANES == 0 else 1
    dims = (count, slabs, n_chan, n_rep, chunks, row_chunks)
    f32, bf16 = jnp.float32, jnp.bfloat16
    dma = pltpu.SemaphoreType.DMA
    anywhere = pl.BlockSpec(memory_space=pl.ANY)
    vmem = pl.BlockSpec(memory_space=pltpu.VMEM)
    return pl.pallas_call(
        functools.partial(kernel, dims),
        in_specs=[anywhere, vmem, vmem, vmem, vmem, anywhere],
        out_specs=vmem,
        out_shape=jax.ShapeDtypeStruct((tok, out_cols // n_rep), bf16),
        scratch_shapes=[
            pltpu.VMEM((3, tok, chans), bf16),
            pltpu.VMEM((3, HALO, chans), bf16),
            pltpu.VMEM((tok + HALO, LANES), f32),
            pltpu.VMEM((BLOCK + modes, WIDE), bf16),
            pltpu.VMEM((tok, chans), f32),
            pltpu.VMEM((tok, chans), f32),
            pltpu.VMEM((count, modes, chans), f32),
            pltpu.VMEM((modes, chans), f32),
            pltpu.VMEM((modes, chans), f32),
            pltpu.VMEM((modes, chans), f32),
            pltpu.VMEM((BLOCK, chans), bf16),
            pltpu.VMEM((n_chan, tok, chans), bf16),
            pltpu.VMEM((count, n_chan, local_rows, out_cols), bf16),
            pltpu.VMEM((tok, out_cols), f32),
            pltpu.VMEM((tok, out_cols // n_rep), f32),
            dma((2,)),
            dma((2,)),
            dma((count,)),
            dma((count,)),
            dma((n_chan,)),
            dma((n_chan,)),
            dma((2, count, chunks)),
            dma((2, count, chunks)),
            dma((2, count, chunks)),
            dma((2, count, chunks)),
            dma((4,)),
            dma((4,)),
        ],
        compiler_params=pltpu.CompilerParams(
            collective_id=0, has_side_effects=True, vmem_limit_bytes=60 * 1024 * 1024
        ),
        name="hyena",
    )(
        projected.transpose(1, 0, 2), short_weight, skip_gain[None], pole_rate, residue, out_weight
    )


def solution(mesh):
    return jax.shard_map(
        per_device,
        mesh=mesh,
        in_specs=(
            P(("groups", "seq"), None, ("chan", "rep")),
            P(None, None, ("chan", "rep")),
            P(("chan", "rep")),
            P(None, ("chan", "rep")),
            P(None, ("chan", "rep")),
            P(None, "rep", "seq", "chan"),
        ),
        out_specs=P(("groups", "seq"), ("chan", "rep")),
        check_vma=False,
    )
```

time: 775 us -> 237 us (0.31)
  waiting for transfers between devices: 353 us -> 0 us
  Pallas kernels: 0 us -> 234 us
  matrix products: 186 us -> 0 us
  local copies, waits for them, and re-layouts: 160 us -> 2.26 us
  other arithmetic: 43.3 us -> 0 us
  between operations: 13.3 us -> 0.01 us
  blocking collectives: 13.2 us -> 0 us
    all_gather x2 -> x0, waiting for transfers between devices: 339 us -> none  [the longest x1 279 us: per_device(): lax.all_gather(out_weight, 'seq', axis=2, tiled=True).reshape(-1, out_cols)]
    pallas_call x0 -> x1, Pallas kernels: none -> 234 us  [per_device(): pl.pallas_call(functools.partial(kernel, dims), in_specs=[anywhere, vmem,...]
    dot_general x15 -> x0, matrix products: 186 us -> none  [the longest x4 141 us: block_step(): inside = jnp.einsum('gij,jgc->igc', kernel, block_in, precision=highest)]
    dynamic_update_slice x4 -> x0, local copies, waits for them, and re-layouts: 106 us -> none  [block_conv(): final_state, outputs = lax.scan(block_step, start_state, blocks_in)]
    convert_element_type x8 -> x0, other arithmetic: 19.9 us -> none  [the longest x1 9.12 us: per_device(): features = projected.astype(jnp.float32)]
    add x1 -> x0, other arithmetic: 18 us -> none  [per_device(): short_weight[:, 0][None] * features]
    reduce_scatter x1 -> x0, waiting for transfers between devices: 14 us -> none  [per_device(): lax.psum_scatter(partial_value, 'rep', scatter_dimension=1, tiled=True)]
    dynamic_slice x4 -> x0, local copies, waits for them, and re-layouts: 13.3 us -> none  [block_conv(): final_state, outputs = lax.scan(block_step, start_state, blocks_in)]
  transfers between devices with their start and end apart: 4 -> 0, of which waited for: 3 -> 0; matrix products, arithmetic and copies ran while one was open for 4% -> 0% of each run, Pallas kernels for 0% -> 0%
where the time goes in v2:
time: 237 us
  Pallas kernels  234 us (99%)
    pallas_call x1, Pallas kernels, per_device(): pl.pallas_call(functools.partial(kernel, dims), in_specs=[anywhere, vmem,...  234 us

profile of v2, /device:TPU:25, one launch (start us, length us, event | category | flops | bytes accessed | tf_op | source)
XLA Modules:
  0.0 236.8 jit_solution(10405139361188748297)
XLA Ops:
  0.0 234.5 %hyena.1 = bf16[512,1024]{1,0:T(8,128)(2,1)} custom-call(bf16[3,512,2048]{2,1,0:T(8,128)(2,1)} %bitcast.2, f32[3,3,2048]{2,1,0:T(4,128)} %sw_ref.1, f32[1,2048]{1,0:T(1,128)} %bitcast.3, f32[16,128]{1,0:T(8,128)} %rate_ref.1, f32[16,128]{1,0:T(8,128)} %res_ref.1, bf16[2,1,512,2048]{3,2,1,0:T(8,128)(2,1)} %w_hbm.1), custom_call_target="tpu_custom_call" | custom-call | tf_op jit(solution)/shard_map/hyena/pallas_call | solution.py:421
  234.5 2.3 copy.8

commit v3 on v2

--- a/solution.py
+++ b/solution.py
@@ -13,6 +13,8 @@
 PER_TILE = LANES // GROUP
 WIDE = PER_TILE * BLOCK
 HALO = 16
+Y_SHARE = 7
+GATE_PARTS = 4
 MESH = pl.DeviceIdType.MESH
 HIGHEST = lax.Precision.HIGHEST
 
@@ -40,6 +42,8 @@
     blocks = tok // BLOCK
     local_rows, out_cols = w_hbm.shape[2], w_hbm.shape[3]
     half = out_cols // slabs
+    y_cols = out_cols // LANES * Y_SHARE // 16 * LANES
+    z_cols = out_cols - y_cols
     rows = local_rows // row_chunks
     out_half = out_cols // n_rep
     slab = lax.axis_index("groups")
@@ -62,8 +66,13 @@
     greet({"rep": other_rep})
     pl.semaphore_wait(barrier, count + n_chan)
 
-    def piece(ref, c, r, h):
-        cols = pl.ds(pl.multiple_of(h * half, LANES), half)
+    def z_span(h):
+        return pl.ds(pl.multiple_of(h * y_cols, LANES), z_cols)
+
+    def y_span(h):
+        return pl.ds(pl.multiple_of(h * z_cols, LANES), y_cols)
+
+    def piece(ref, c, r, cols):
         if chunks == 1:
             return ref.at[:, :, cols]
         return ref.at[c, pl.ds(pl.multiple_of(r * rows, rows), rows), cols]
@@ -73,11 +82,11 @@
 
     def own_piece(ch):
         c, r = split(ch)
-        return piece(w_hbm.at[:, 0], c, r, slab)
-
-    def block_piece(b, ch, h):
+        return piece(w_hbm.at[:, 0], c, r, z_span(slab))
+
+    def block_piece(b, ch, cols):
         c, r = split(ch)
-        return piece(wbuf.at[b], c, r, h)
+        return piece(wbuf.at[b], c, r, cols)
 
     def target_of(direction):
         return seq + 1 if direction == 0 else seq - 1
@@ -93,14 +102,14 @@
 
     def z_copy(direction, k, ch, src, b):
         return pltpu.make_async_remote_copy(
-            src_ref=src, dst_ref=block_piece(b, ch, slab),
+            src_ref=src, dst_ref=block_piece(b, ch, z_span(slab)),
             send_sem=zsend.at[direction, k, ch], recv_sem=zrecv.at[direction, k, ch],
             device_id={"seq": target_of(direction)}, device_id_type=MESH,
         )
 
     def y_copy(direction, k, ch, h):
         b = origin(direction, k)
-        ref = block_piece(b, ch, h)
+        ref = block_piece(b, ch, y_span(h))
         return pltpu.make_async_remote_copy(
             src_ref=ref, dst_ref=ref,
             send_sem=ysend.at[direction, k, ch], recv_sem=yrecv.at[direction, k, ch],
@@ -143,13 +152,14 @@
             @pl.when(has(direction, k))
             def _():
                 b = origin(direction, k)
-                landed = block_piece(b, ch, slab)
+                landed = block_piece(b, ch, z_span(slab))
                 z_copy(direction, k, ch, landed, b).wait_recv()
-                y_copy(direction, k, ch, slab).start()
 
                 @pl.when(can_send(direction))
                 def _():
                     z_copy(direction, k + 1, ch, landed, b).start()
+
+                y_copy(direction, k, ch, slab).start()
 
     def conv_tile(t, carry):
         cols = pl.ds(pl.multiple_of(t * LANES, LANES), LANES)
@@ -221,7 +231,8 @@
         return carry
 
     steps = [(k, ch) for k in range(count - 1) for ch in range(chunks)]
-    early = 3 if len(steps) > 3 and chunks >= 3 else 1
+    total = len(steps)
+    early = 1
     part = tiles // (early + 1)
     for e in range(early + 1):
         stop = tiles if e == early else (e + 1) * part
@@ -248,6 +259,7 @@
         def _():
             end_copy(d).start()
 
+    pump(*steps[early])
     prior[...] = jnp.zeros_like(prior)
     for source in range(count - 1):
         @pl.when(source < seq)
@@ -271,33 +283,38 @@
             state = decay * state
         return carry
 
-    lax.fori_loop(0, tiles, gate_tile, 0)
-
-    def gate_copy(d):
-        return pltpu.make_async_remote_copy(
-            src_ref=gated.at[chan], dst_ref=gated.at[chan],
-            send_sem=gate_send.at[d], recv_sem=gate_recv.at[chan],
+    share = chans // GATE_PARTS
+
+    def gate_copy(d, i):
+        part_ref = gated.at[chan, :, pl.ds(i * share, share)]
+        return pltpu.make_async_remote_copy(
+            src_ref=part_ref, dst_ref=part_ref,
+            send_sem=gate_send.at[d, i], recv_sem=gate_recv.at[chan, i],
             device_id={"chan": lax.rem(chan + d, n_chan)}, device_id_type=MESH,
         )
 
-    def arrived_gate(d):
+    def arrived_gate(d, i):
         source = lax.rem(chan + d, n_chan)
-        return pltpu.make_async_remote_copy(
-            src_ref=gated.at[source], dst_ref=gated.at[source],
-            send_sem=gate_send.at[0], recv_sem=gate_recv.at[source],
+        part_ref = gated.at[source, :, pl.ds(i * share, share)]
+        return pltpu.make_async_remote_copy(
+            src_ref=part_ref, dst_ref=part_ref,
+            send_sem=gate_send.at[0, i], recv_sem=gate_recv.at[source, i],
             device_id={"chan": source}, device_id_type=MESH,
         )
 
-    for d in range(1, n_chan):
-        gate_copy(d).start()
-
-    middle = min(len(steps), early + 3)
-    for e in range(early, middle):
+    for i in range(GATE_PARTS):
+        lax.fori_loop(i * tiles // GATE_PARTS, (i + 1) * tiles // GATE_PARTS, gate_tile, 0)
+        for d in range(1, n_chan):
+            gate_copy(d, i).start()
+
+    middle = max(min(2, total), total * 2 // 3)
+    for e in range(early + 1, middle):
         pump(*steps[e])
     acc[...] = jnp.zeros_like(acc)
     w_copy.wait()
     for d in range(1, n_chan):
-        arrived_gate(d).wait_recv()
+        for i in range(GATE_PARTS):
+            arrived_gate(d, i).wait_recv()
 
     streamed = chunks > 1
     col_tile = min(512, out_cols)
@@ -322,23 +339,33 @@
                 if streamed:
                     multiply(origin(direction, k), ch)
 
-    if streamed:
-        lax.fori_loop(0, chunks, lambda ch, carry: (multiply(seq, ch), carry)[1], 0)
+    left_over = total - middle
+    own_per = -(-chunks // left_over)
+    per = -(-total // left_over)
 
     def both(j, carry):
         pump(j // chunks, j % chunks)
-        old = j - 1
-        consume(old // chunks, old % chunks)
+        if streamed:
+            for i in range(own_per):
+                ch = (j - middle) * own_per + i
+
+                @pl.when(ch < chunks)
+                def _():
+                    multiply(seq, ch)
+
+        def late(i, inner):
+            old = (j - middle) * per + i
+
+            @pl.when(old < total)
+            def _():
+                consume(old // chunks, old % chunks)
+
+            return inner
+
+        lax.fori_loop(0, per, late, 0)
         return carry
 
-    def only(j, carry):
-        consume(j // chunks, j % chunks)
-        return carry
-
-    total = len(steps)
-    lax.fori_loop(0, middle - 1, only, 0)
     lax.fori_loop(middle, total, both, 0)
-    lax.fori_loop(total - 1, total, only, 0)
 
     if not streamed:
         def whole_column(n, carry):
@@ -373,7 +400,8 @@
     for i in range(4):
         rep_copy(i, other_rep).wait_send()
     for d in range(1, n_chan):
-        gate_copy(d).wait_send()
+        for i in range(GATE_PARTS):
+            gate_copy(d, i).wait_send()
     for d in range(1, count):
         @pl.when(seq + d < count)
         def _():
@@ -399,7 +427,7 @@
                 @pl.when(can_send(direction))
                 def _():
                     b = origin(direction, k)
-                    z_copy(direction, k + 1, ch, block_piece(b, ch, slab), b).wait_send()
+                    z_copy(direction, k + 1, ch, block_piece(b, ch, z_span(slab)), b).wait_send()
         return carry
 
     lax.fori_loop(0, total, drain, 0)
@@ -443,8 +471,8 @@
             dma((2,)),
             dma((count,)),
             dma((count,)),
-            dma((n_chan,)),
-            dma((n_chan,)),
+            dma((n_chan, GATE_PARTS)),
+            dma((n_chan, GATE_PARTS)),
             dma((2, count, chunks)),
             dma((2, count, chunks)),
             dma((2, count, chunks)),

time: 237 us -> 197 us (0.83)
  Pallas kernels: 234 us -> 194 us
    pallas_call x1, Pallas kernels: 234 us -> 194 us  [per_device(): pl.pallas_call(functools.partial(kernel, dims), in_specs=[anywhere, vmem,...]
where the time goes in v3:
time: 197 us
  Pallas kernels  194 us (98%)
  local copies, waits for them, and re-layouts  2.26 us (1%)
    pallas_call x1, Pallas kernels, per_device(): pl.pallas_call(functools.partial(kernel, dims), in_specs=[anywhere, vmem,...  194 us

profile of v3, /device:TPU:25, one launch (start us, length us, event | category | flops | bytes accessed | tf_op | source)
XLA Modules:
  0.0 196.8 jit_solution(17248804271107460079)
XLA Ops:
  0.0 194.5 %hyena.1 = bf16[512,1024]{1,0:T(8,128)(2,1)} custom-call(bf16[3,512,2048]{2,1,0:T(8,128)(2,1)} %bitcast.2, f32[3,3,2048]{2,1,0:T(4,128)} %sw_ref.1, f32[1,2048]{1,0:T(1,128)} %bitcast.3, f32[16,128]{1,0:T(8,128)} %rate_ref.1, f32[16,128]{1,0:T(8,128)} %res_ref.1, bf16[2,1,512,2048]{3,2,1,0:T(8,128)(2,1)} %w_hbm.1), custom_call_target="tpu_custom_call" | custom-call | tf_op jit(solution)/shard_map/hyena/pallas_call | solution.py:449
  194.5 2.3 %copy.8 = bf16[512,1024]{1,0:T(8,128)(2,1)} copy(bf16[512,1024]{1,0:T(8,128)(2,1)} %hyena.1) | data formatting | bytes 2097152
